TPU v7x, 32 devices: a whole 2x2x4 slice. The times are simulated.
32 devices in a mesh: teacher: 4 (over y, x), student: 8 (over z, core).
Axes of the slice: x: 2, y: 2, z: 4, core: 2. Of those that a mesh axis runs over, the one named last changes fastest.
Arguments:
- teacher_in: bfloat16 [8192, 8192], P('student', 'teacher')
- teacher_attn: bfloat16 [8192, 4096], P('student', 'teacher'), may hold values from -6 to 6
- teacher_out_proj: bfloat16 [4096, 8192], P('student', 'teacher'), may hold values from -0.09375 to 0.09375
- teacher_gain: bfloat16 [8192], P('teacher'), may hold values from 0.099609375 to 1.8984375
- projection: bfloat16 [8192, 4096], P('teacher', 'student'), may hold values from -0.0625 to 0.0625
- student_in: bfloat16 [8192, 4096], P('student', 'teacher')
- student_attn: bfloat16 [8192, 2048], P('student', 'teacher'), may hold values from -6 to 6
- student_out_proj: bfloat16 [2048, 4096], P('student', 'teacher'), may hold values from -0.125 to 0.125
- student_gain: bfloat16 [4096], P('teacher'), may hold values from 0.099609375 to 1.8984375
- token_ids: int32 [8192], P('student'), may hold values from 0 to 128004, as said below
- row_order: int32 [8192], replicated, may hold values from 0 to 8191, as said below
Outputs:
- grad_weight: float32 [2048, 4096], P('student', 'teacher')
- grad_gain: float32 [4096], P('teacher')
Inputs may be any that keep to these rules, and one draw needn't show every extreme that they name: `token_ids`: within each sequence of 1024 consecutive rows the rows holding 128004 form the sequence's tail, after at least 256 other rows; no other row holds 128004. `row_order`: A permutation of the 8192 rows. For student block k and teacher block b (blocks of 1024 rows), the entries k * 1024 + b * 128 to k * 1024 + (b + 1) * 128 - 1 name rows of teacher block b.
All inputs are finite; a program needn't handle non-finite values.
Results may differ from a plain program's by a relative error of at most 0.02.
Values may be sent and summed in bfloat16 or wider, within the bound.
No kernel may reach another device: no remote copies, remote signals or barrier semaphores. Data moves between devices by JAX's collectives and lax.ppermute only.
A program may use at most 128 MiB of HBM per device.

v0:
```python
import math
import jax
import jax.numpy as jnp
from jax import lax
from jax.sharding import PartitionSpec as P

DT = 8192
DS = 4096
PAD_ID = 128004
epsilon = 1e-05


def shards(
    teacher_in,
    teacher_attn,
    teacher_out_proj,
    teacher_gain,
    projection,
    student_in,
    student_attn,
    student_out_proj,
    student_gain,
    token_ids,
    row_order,
):
    student_count = lax.axis_size("student")
    teacher_count = lax.axis_size("teacher")
    row_count = teacher_in.shape[0]
    piece_rows = row_count // student_count
    student_index = lax.axis_index("student")
    attn_all = lax.all_gather(teacher_attn, "teacher", axis=1, tiled=True)
    columns = attn_all
    branch = jnp.dot(
        columns,
        lax.all_gather(teacher_out_proj, "student", axis=0, tiled=True),
        preferred_element_type=jnp.float32,
    )
    proj_full = lax.all_gather(projection, "student", axis=1, tiled=True)
    residual = teacher_in.astype(jnp.float32) + branch
    square_sum = lax.psum(jnp.sum(residual * residual, axis=1), "teacher")
    teacher_scale = lax.rsqrt(square_sum / DT + epsilon)
    hidden = (residual * teacher_scale[:, None] * teacher_gain.astype(jnp.float32)[None, :]).astype(
        jnp.bfloat16
    )
    proj_blocks = proj_full.reshape(
        proj_full.shape[0], teacher_count, proj_full.shape[1] // teacher_count
    )
    row_blocks = row_order.reshape(student_count, student_count, piece_rows)
    local_rows = (
        lax.dynamic_index_in_dim(row_blocks, student_index, 1, keepdims=False)
        - student_index * row_count
    )
    live_rows = jnp.where(token_ids != PAD_ID, 1.0, 0.0).astype(jnp.bfloat16)
    mask_send = jnp.take(live_rows, local_rows, axis=0)
    columns = proj_blocks
    summed = lax.psum_scatter(
        jnp.einsum("tf,fko->kto", hidden, columns, preferred_element_type=jnp.float32).astype(
            jnp.bfloat16
        ),
        "teacher",
        scatter_dimension=0,
        tiled=True,
    ).astype(jnp.float32)
    target_rows = summed[0].astype(jnp.bfloat16)
    moved, mask_got = (
        lax.all_to_all(
            jnp.take(target_rows, local_rows, axis=0),
            "student",
            split_axis=0,
            concat_axis=0,
            tiled=True,
        ),
        lax.all_to_all(mask_send, "student", split_axis=0, concat_axis=0, tiled=True),
    )
    target = moved.reshape(row_count, moved.shape[2])
    weight_mask = mask_got.reshape(row_count).astype(jnp.float32)
    attn_student = lax.all_gather(student_attn, "teacher", axis=1, tiled=True)
    columns = attn_student
    student_branch = jnp.dot(
        columns,
        lax.all_gather(student_out_proj, "student", axis=0, tiled=True),
        preferred_element_type=jnp.float32,
    )
    student_res = student_in.astype(jnp.float32) + student_branch
    student_square = lax.psum(jnp.sum(student_res * student_res, axis=1), "teacher")
    student_scale = lax.rsqrt(student_square / DS + epsilon)
    normed = student_res * student_scale[:, None]
    gain_values = student_gain.astype(jnp.float32)[None, :]
    distance = normed * gain_values - target.astype(jnp.float32)
    loss_weight = 1.0 / math.sqrt(row_count * student_count)
    grad_out = distance * (weight_mask * loss_weight)[:, None]
    gain_part = jnp.sum(grad_out * normed, axis=0)
    grad_norm = grad_out * gain_values
    inner_sum = lax.psum(jnp.sum(grad_norm * normed, axis=1), "teacher")
    grad_res = (student_scale[:, None] * (grad_norm - normed * (inner_sum / DS)[:, None])).astype(
        jnp.bfloat16
    )
    columns = attn_student
    grad_weight = lax.psum_scatter(
        lax.dot_general(
            columns, grad_res, (((0,), (0,)), ((), ())), preferred_element_type=jnp.float32
        ).astype(jnp.bfloat16),
        "student",
        scatter_dimension=0,
        tiled=True,
    ).astype(jnp.float32)
    grad_gain = lax.psum(gain_part, "student")
    return (grad_weight, grad_gain)


def solution(mesh):
    placed = (
        P("student", "teacher"),
        P("student", "teacher"),
        P("student", "teacher"),
        P("teacher"),
        P("teacher", "student"),
        P("student", "teacher"),
        P("student", "teacher"),
        P("student", "teacher"),
        P("teacher"),
        P("student"),
        P(),
    )
    return jax.shard_map(
        shards,
        mesh=mesh,
        in_specs=placed,
        out_specs=(P("student", "teacher"), P("teacher")),
        check_vma=False,
    )
```

profile of v0, /device:TPU:0, one launch (start us, length us, event | category | flops | bytes accessed | tf_op | source)
XLA Modules:
  0.0 761.1 jit_solution(17488649339242364918)
XLA Ops:
  7.2 0.7 all-gather.6.cloned.1.call-update
  8.0 0.7 all-gather.8.cloned.1.call-update
  8.7 0.7 all-gather.10.cloned.1.call-update
  9.4 0.5 all-gather.12.cloned.1.call-update
  10.0 2.5 copy.28
  12.6 0.0 reduce-scatter.7.cloned.1.call-start
  12.6 2.9 copy.27
  15.5 49.5 %all-gather.6.cloned.1.call-done = bf16[1024,2048]{1,0:T(8,128)(2,1)} async-done(((bf16[1024,512]{1,0:T(8,128)(2,1)}), bf16[1024,2048]{1,0:T(8,128)(2,1)}) %all-gather.6.cloned.1.call-update) | async-done | bytes 4194320 | tf_op jit(solution)/shard_map/all_gather | solution.py:77
  65.0 48.5 %all-gather.8.cloned.1.call-done = bf16[2048,1024]{1,0:T(8,128)(2,1)} async-done(((bf16[256,1024]{1,0:T(8,128)(2,1)}), bf16[2048,1024]{1,0:T(8,128)(2,1)}) %all-gather.8.cloned.1.call-update) | async-done | bytes 4194320 | tf_op jit(solution)/shard_map/all_gather | solution.py:81
  113.5 10.3 %multiply_reduce_fusion.3 = (f32[1024]{0:T(1024)S(1)}, f32[1024,1024]{0,1:T(8,128)}) fusion(bf16[1024,2048]{1,0:T(8,128)(2,1)} %all-gather.6.cloned.1.call-done, bf16[2048,1024]{1,0:T(8,128)(2,1)} %all-gather.8.cloned.1.call-done, bf16[1024,1024]{0,1:T(8,128)(2,1)S(1)} %copy.27), kind=kOutput, calls=%fused_computation.16 | convolution fusion | flops 4299160576 | bytes 14684160 | tf_op jit(solution)/shard_map/dot_general | solution.py:79
  123.8 77.9 %all-gather.10.cloned.1.call-done = bf16[1024,4096]{1,0:T(8,128)(2,1)} async-done(((bf16[1024,1024]{1,0:T(8,128)(2,1)}), bf16[1024,4096]{1,0:T(8,128)(2,1)}) %all-gather.10.cloned.1.call-update) | async-done | bytes 8388624 | tf_op jit(solution)/shard_map/all_gather | solution.py:31
  201.7 152.6 %all-gather.12.cloned.1.call-done = bf16[4096,2048]{1,0:T(8,128)(2,1)} async-done(((bf16[512,2048]{1,0:T(8,128)(2,1)}), bf16[4096,2048]{1,0:T(8,128)(2,1)}) %all-gather.12.cloned.1.call-update) | async-done | bytes 16777232 | tf_op jit(solution)/shard_map/all_gather | solution.py:35
  354.2 24.6 %multiply_reduce_fusion = (f32[1024]{0:T(1024)S(1)}, f32[1024,2048]{1,0:T(8,128)}) fusion(bf16[1024,2048]{1,0:T(8,128)(2,1)} %param.11, bf16[1024,4096]{1,0:T(8,128)(2,1)} %all-gather.10.cloned.1.call-done, bf16[4096,2048]{1,0:T(8,128)(2,1)} %all-gather.12.cloned.1.call-done), kind=kOutput, calls=%fused_computation.4 | convolution fusion | flops 17188257792 | bytes 37752832 | tf_op jit(solution)/shard_map/dot_general | solution.py:33
  378.8 10.2 %all-reduce.1 = (f32[1024]{0:T(1024)S(1)}, f32[1024]{0:T(1024)S(1)}) all-reduce(f32[1024]{0:T(1024)S(1)} %get-tuple-element.14, f32[1024]{0:T(1024)S(1)} %get-tuple-element.16), channel_id=1, replica_groups=mesh['teacher'=4,'student'=8] {'teacher'}, use_global_device_ids=true, to_apply=%region_3.4 | all-reduce | flops 2048 | bytes 16384 | tf_op jit(solution)/shard_map/psum | solution.py:40
  389.0 116.0 %all-gather.14.cloned.1.call-done = bf16[2048,4096]{0,1:T(8,128)(2,1)} async-done(((bf16[2048,512]{0,1:T(8,128)(2,1)}), bf16[2048,4096]{0,1:T(8,128)(2,1)}) %all-gather.14.cloned.1.call-update) | async-done | bytes 16777232 | tf_op jit(solution)/shard_map/all_gather | solution.py:38
  505.0 25.5 %convert_bitcast_fusion = bf16[4,1024,1024]{2,1,0:T(8,128)(2,1)} fusion(bf16[2048,4,1024]{0,2,1:T(8,128)(2,1)} %bitcast.51, f32[1024,2048]{1,0:T(8,128)} %get-tuple-element.15, bf16[1024,2048]{1,0:T(8,128)(2,1)} %param.11, f32[2048]{0:T(1024)S(1)} %convert_element_type.58, f32[1024]{0:T(1024)S(1)} %add_rsqrt_fusion), kind=kOutput, calls=%fused_computation.2 | convolution fusion | flops 17194549248 | bytes 37761024 | tf_op jit(solution)/shard_map/tf,fko->kto/dot_general | solution.py:57
  530.5 0.8 dynamic-slice_subtract_fusion
  531.3 6.8 gather_fusion.1
  538.1 1.4 and_select_fusion
  539.5 3.3 all-to-all-start.1
  542.8 72.3 %reduce-scatter.7.cloned.1.call-done = bf16[1,1024,1024]{2,1,0:T(8,128)(2,1)} async-done(((bf16[4,1024,1024]{2,1,0:T(8,128)(2,1)}), bf16[1,1024,1024]{2,1,0:T(8,128)(2,1)}) %reduce-scatter.7.cloned.1.call-update) | async-done | bytes 2097168
  615.2 6.8 gather_fusion
  622.0 2.4 copy.30
  624.4 3.2 broadcast_select_fusion
  627.6 4.6 all-to-all-start
  632.2 48.9 %all-to-all-done = bf16[8,128,1024]{1,2,0:T(8,128)(2,1)S(1)} async-done(((bf16[8,128,1024]{1,2,0:T(8,128)(2,1)}), bf16[8,128,1024]{1,2,0:T(8,128)(2,1)S(1)}, u32[]{:S(2)}, u32[]{:S(2)}) %all-to-all-start) | async-done | bytes 2097184 | tf_op jit(solution)/shard_map/all_to_all | solution.py:66
  681.2 3.5 multiply_reduce_fusion.1
  684.7 9.0 %psum.30 = f32[1024]{0:T(1024)S(1)} all-reduce(f32[1024]{0:T(1024)S(1)} %get-tuple-element.11), channel_id=1, replica_groups=mesh['teacher'=4,'student'=8] {'teacher'}, use_global_device_ids=true, to_apply=%region_6.7 | all-reduce | flops 1024 | bytes 8192 | tf_op jit(solution)/shard_map/psum | solution.py:94
  693.6 10.3 %convert_bitcast_fusion.2 = bf16[2048,1024]{0,1:T(8,128)(2,1)} fusion(bf16[1024,2048]{1,0:T(8,128)(2,1)} %all-gather.6.cloned.1.call-done, f32[1024,1024]{0,1:T(8,128)} %get-tuple-element.17, f32[1024]{0:T(1024)S(1)} %broadcast_multiply_fusion, f32[1024]{0:T(1024)S(1)} %bitcast.47, f32[1024]{0:T(1024)S(1)} %convert_element_type.56, ...), kind=kOutput, calls=%fused_computation.11 | convolution fusion | flops 4307550208 | bytes 14696448 | tf_op jit(solution)/shard_map/dot_general | solution.py:100
  703.9 14.7 %psum.31 = f32[1024]{0:T(1024)} all-reduce(f32[1024]{0:T(1024)S(1)} %get-tuple-element.10), channel_id=1, replica_groups=mesh['teacher'=4,'student'=8] {'student'}, use_global_device_ids=true, to_apply=%region_9.10 | all-reduce | flops 1024 | bytes 8192 | tf_op jit(solution)/shard_map/psum | solution.py:107
  718.6 33.4 %reduce-scatter.5.cloned.1.call-done = bf16[256,1024]{0,1:T(8,128)(2,1)} async-done(((bf16[2048,1024]{0,1:T(8,128)(2,1)}), bf16[256,1024]{0,1:T(8,128)(2,1)}) %reduce-scatter.5.cloned.1.call-update) | async-done | bytes 524304 | tf_op jit(solution)/shard_map/reduce_scatter | solution.py:99
  752.1 2.2 copy.33
  (27 shorter events, 0.3 us)
Async XLA Ops:
  7.2 2.9 copy-start
  7.2 57.8 %all-gather.6.cloned.1.call-start = ((), (), s32[]{:S(2)}) async-start(), calls=%async_computation.4 | async-start | bytes 5242880 | tf_op jit(solution)/shard_map/all_gather | solution.py:77
  7.9 105.6 %all-gather.8.cloned.1.call-start = ((), (), s32[]{:S(2)}) async-start(), calls=%async_computation.5 | async-start | bytes 4718592 | tf_op jit(solution)/shard_map/all_gather | solution.py:81
  8.7 193.0 %all-gather.10.cloned.1.call-start = ((), (), s32[]{:S(2)}) async-start(), calls=%async_computation.6 | async-start | bytes 10485760 | tf_op jit(solution)/shard_map/all_gather | solution.py:31
  9.4 344.8 %all-gather.12.cloned.1.call-start = ((), (), s32[]{:S(2)}) async-start(), calls=%async_computation.7 | async-start | bytes 18874368 | tf_op jit(solution)/shard_map/all_gather | solution.py:35
  10.0 495.0 %all-gather.14.cloned.1.call-start = ((), (), s32[]{:S(2)}) async-start(), calls=%async_computation.8 | async-start | bytes 18874368 | tf_op jit(solution)/shard_map/all_gather | solution.py:38
  12.6 2.9 copy-start.1
  12.6 602.6 %reduce-scatter.7.cloned.1.call-start = ((), (), s32[]{:S(2)}) async-start(), calls=%async_computation.10 | async-start | bytes 10485760
  530.5 0.8 copy-start.2
  539.5 88.1 %all-to-all-start.1 = ((bf16[8,1,128]{2,1,0:T(2,128)(2,1)}), bf16[8,1,128]{2,1,0:T(2,128)(2,1)S(1)}, u32[]{:S(2)}, u32[]{:S(2)}) async-start(bf16[8,1,128]{2,1,0:T(2,128)(2,1)} %and_select_fusion), calls=%async_computation.1 | async-start | bytes 8192 | tf_op jit(solution)/shard_map/all_to_all | solution.py:73
  624.4 7.8 %copy-start.3 = (bf16[1024]{0:T(1024)(128)(2,1)S(1)}, bf16[1024]{0:T(1024)(128)(2,1)}, u32[]{:S(2)}) copy-start(bf16[1024]{0:T(1024)(128)(2,1)} %param.19) | copy-start | bytes 6148
  627.6 53.6 %all-to-all-start = ((bf16[8,128,1024]{1,2,0:T(8,128)(2,1)}), bf16[8,128,1024]{1,2,0:T(8,128)(2,1)S(1)}, u32[]{:S(2)}, u32[]{:S(2)}) async-start(bf16[8,128,1024]{1,2,0:T(8,128)(2,1)} %broadcast_select_fusion), calls=%async_computation | async-start | bytes 4194304 | tf_op jit(solution)/shard_map/all_to_all | solution.py:66
  632.2 119.9 %reduce-scatter.5.cloned.1.call-start = ((), (), s32[]{:S(2)}) async-start(), calls=%async_computation.9 | async-start | bytes 4718592 | tf_op jit(solution)/shard_map/reduce_scatter | solution.py:99
Sparse Core Ops, SparseCore 0:
  9.8 55.1 all-gather.5
  66.6 46.8 all-gather.7
  115.4 86.2 all-gather.9
  203.1 151.0 all-gather.11
  355.7 149.2 all-gather.13
  530.6 84.5 reduce-scatter.6
  704.0 47.9 reduce-scatter.4
where the time goes:
time: 762 us; the launch traced here: 761 us
  waiting for transfers between devices  602 us (79%)
  matrix products  70.6 us (9%)
  blocking collectives  33.8 us (4%)
  local copies, waits for them, and re-layouts  23.7 us (3%)
  between operations  14.3 us (2%)
  other arithmetic  8.85 us (1%)
  starting transfers between devices  8.17 us (1%)
    all_gather x1, waiting for transfers between devices, shards(): lax.all_gather(teacher_out_proj, 'student', axis=0, tiled=True)  153 us
    all_gather x1, waiting for transfers between devices, shards(): proj_full = lax.all_gather(projection, 'student', axis=1, tiled=True)  116 us
    all_gather x1, waiting for transfers between devices, shards(): attn_all = lax.all_gather(teacher_attn, 'teacher', axis=1, tiled=True)  77.9 us
    unnamed x8, waiting for transfers between devices  75 us
    all_gather x1, waiting for transfers between devices, shards(): attn_student = lax.all_gather(student_attn, 'teacher', axis=1, tiled=True)  49.5 us
    all_to_all x1, waiting for transfers between devices, shards(): lax.all_to_all(jnp.take(target_rows, local_rows, axis=0), 'student', spli...  48.9 us
    all_gather x1, waiting for transfers between devices, shards(): lax.all_gather(student_out_proj, 'student', axis=0, tiled=True)  48.5 us
    reduce_scatter x1, waiting for transfers between devices, shards(): lax.psum_scatter(lax.dot_general(columns, grad_res, (((0,), (0,)), ((), (...  33.4 us
  transfers between devices with their start and end apart: 9, of which 8 were waited for; matrix products, arithmetic and copies ran while one was open for 8% of the time, Pallas kernels for 0%

commit v1 on v0

--- a/solution.py
+++ b/solution.py
@@ -8,6 +8,12 @@
 DS = 4096
 PAD_ID = 128004
 epsilon = 1e-05
+
+
+def meet_ports(frame, row_dim):
+    val = list(frame.shape[1:])
+    val[row_dim] *= frame.shape[0]
+    return jnp.moveaxis(frame, 0, row_dim).reshape(val)
 
 
 def shards(
@@ -74,7 +80,31 @@
     )
     target = moved.reshape(row_count, moved.shape[2])
     weight_mask = mask_got.reshape(row_count).astype(jnp.float32)
-    attn_student = lax.all_gather(student_attn, "teacher", axis=1, tiled=True)
+    crops = []
+    nodes = lax.axis_size("teacher")
+    for num in range(nodes):
+        crops.append((num, (num + 1) % nodes))
+    all_blocks = []
+    for idx, s in crops:
+        all_blocks.append((s, idx))
+    b_next, main = ([], [])
+    for j0 in range(nodes - 1):
+        if j0 % 2 == 0:
+            b_next.append(
+                lax.ppermute(
+                    b_next[-1] if b_next else student_attn, axis_name="teacher", perm=crops
+                )
+            )
+        else:
+            main.append(
+                lax.ppermute(
+                    main[-1] if main else student_attn, axis_name="teacher", perm=all_blocks
+                )
+            )
+    local_next = jnp.stack([*b_next[::-1], student_attn, *main])
+    value_now = lax.axis_index("teacher") - len(b_next)
+    local_next = local_next[(jnp.arange(nodes) - value_now) % nodes]
+    attn_student = meet_ports(local_next, 1)
     columns = attn_student
     student_branch = jnp.dot(
         columns,

time: 762 us -> 720 us (0.945)
  waiting for transfers between devices: 602 us -> 539 us
  local copies, waits for them, and re-layouts: 23.7 us -> 32.6 us
    ppermute x0 -> x3, waiting for transfers between devices: none -> 76.5 us  [the longest x2 57.5 us: shards(): lax.ppermute(b_next[-1] if b_next else student_attn, axis_name='teacher',...]
    all_gather x1 -> x0, waiting for transfers between devices: 49.5 us -> none  [shards(): attn_student = lax.all_gather(student_attn, 'teacher', axis=1, tiled=True)]
    all_gather x1, waiting for transfers between devices: 48.5 us -> 0.01 us  [shards(): lax.all_gather(student_out_proj, 'student', axis=0, tiled=True)]
    all_gather x1, waiting for transfers between devices: 77.9 us -> 36.9 us  [shards(): attn_all = lax.all_gather(teacher_attn, 'teacher', axis=1, tiled=True)]
    unnamed x8 -> x7, waiting for transfers between devices: 75 us -> 74.4 us
  transfers between devices with their start and end apart: 9 -> 11, of which waited for: 8 -> 9; matrix products, arithmetic and copies ran while one was open for 8% -> 11% of each run, Pallas kernels for 0% -> 0%
where the time goes in v1:
time: 720 us
  waiting for transfers between devices  539 us (75%)
  matrix products  72.2 us (10%)
  blocking collectives  33.8 us (5%)
  local copies, waits for them, and re-layouts  32.6 us (5%)
  other arithmetic  14.6 us (2%)
  between operations  14.3 us (2%)
  starting transfers between devices  13.3 us (2%)
    all_gather x1, waiting for transfers between devices, shards(): lax.all_gather(teacher_out_proj, 'student', axis=0, tiled=True)  153 us
    all_gather x1, waiting for transfers between devices, shards(): proj_full = lax.all_gather(projection, 'student', axis=1, tiled=True)  116 us
    unnamed x7, waiting for transfers between devices  74.4 us
    ppermute x2, waiting for transfers between devices, shards(): lax.ppermute(b_next[-1] if b_next else student_attn, axis_name='teacher',...  57.5 us
    all_to_all x1, waiting for transfers between devices, shards(): lax.all_to_all(jnp.take(target_rows, local_rows, axis=0), 'student', spli...  48.9 us
    all_gather x1, waiting for transfers between devices, shards(): attn_all = lax.all_gather(teacher_attn, 'teacher', axis=1, tiled=True)  36.9 us
    reduce_scatter x1, waiting for transfers between devices, shards(): lax.psum_scatter(lax.dot_general(columns, grad_res, (((0,), (0,)), ((), (...  33.4 us
    dot_general x1, matrix products, shards(): jnp.einsum('tf,fko->kto', hidden, columns, preferred_element_type=jnp.flo...  25.5 us
  transfers between devices with their start and end apart: 11, of which 9 were waited for; matrix products, arithmetic and copies ran while one was open for 11% of the time, Pallas kernels for 0%

profile of v1, /device:TPU:0, one launch (start us, length us, event | category | flops | bytes accessed | tf_op | source)
XLA Modules:
  0.0 719.7 jit_solution(12687186710752636529)
XLA Ops:
  9.5 2.5 copy.27
  12.0 3.0 collective-permute-start
  16.0 24.0 %collective-permute-done = bf16[1024,512]{1,0:T(8,128)(2,1)} collective-permute-done((bf16[1024,512]{1,0:T(8,128)(2,1)S(1)}, bf16[1024,512]{1,0:T(8,128)(2,1)}, u32[]{:S(2)}, u32[]{:S(2)}) %collective-permute-start) | collective-permute-done | bytes 1048608 | tf_op jit(solution)/shard_map/ppermute | solution.py:94
  40.1 1.1 collective-permute-start.1
  41.2 2.9 copy.26
  44.1 19.0 %collective-permute-done.2 = bf16[1024,512]{1,0:T(8,128)(2,1)} collective-permute-done((bf16[1024,512]{1,0:T(8,128)(2,1)S(1)}, bf16[1024,512]{1,0:T(8,128)(2,1)}, u32[]{:S(2)}, u32[]{:S(2)}) %collective-permute-start.2) | collective-permute-done | bytes 1048608 | tf_op jit(solution)/shard_map/ppermute | solution.py:100
  63.1 33.5 %collective-permute-done.1 = bf16[1024,512]{1,0:T(8,128)(2,1)} collective-permute-done((bf16[1024,512]{1,0:T(8,128)(2,1)}, bf16[1024,512]{1,0:T(8,128)(2,1)}, u32[]{:S(2)}, u32[]{:S(2)}) %collective-permute-start.1) | collective-permute-done | bytes 1048608 | tf_op jit(solution)/shard_map/ppermute | solution.py:94
  96.6 3.6 pad_maximum_fusion
  100.1 5.0 gather_fusion
  105.1 6.3 copy.25
  111.4 11.6 %multiply_reduce_fusion.3 = (f32[1024]{0:T(1024)S(1)}, f32[1024,1024]{0,1:T(8,128)}) fusion(bf16[1024,2048]{0,1:T(8,128)(2,1)} %bitcast.51, bf16[2048,1024]{1,0:T(8,128)(2,1)} %all-gather.5.cloned.1.call-done, bf16[1024,1024]{0,1:T(8,128)(2,1)S(1)} %copy.26), kind=kOutput, calls=%fused_computation.17 | convolution fusion | flops 4299160576 | bytes 14684160 | tf_op jit(solution)/shard_map/dot_general | solution.py:109
  123.0 36.9 %all-gather.7.cloned.1.call-done = bf16[1024,4096]{1,0:T(8,128)(2,1)} async-done(((bf16[1024,1024]{1,0:T(8,128)(2,1)}), bf16[1024,4096]{1,0:T(8,128)(2,1)}) %all-gather.7.cloned.1.call-update) | async-done | bytes 8388624 | tf_op jit(solution)/shard_map/all_gather | solution.py:37
  159.9 152.7 %all-gather.9.cloned.1.call-done = bf16[4096,2048]{1,0:T(8,128)(2,1)} async-done(((bf16[512,2048]{1,0:T(8,128)(2,1)}), bf16[4096,2048]{1,0:T(8,128)(2,1)}) %all-gather.9.cloned.1.call-update) | async-done | bytes 16777232 | tf_op jit(solution)/shard_map/all_gather | solution.py:41
  312.7 24.6 %multiply_reduce_fusion = (f32[1024]{0:T(1024)S(1)}, f32[1024,2048]{1,0:T(8,128)}) fusion(bf16[1024,2048]{1,0:T(8,128)(2,1)} %param.11, bf16[1024,4096]{1,0:T(8,128)(2,1)} %all-gather.7.cloned.1.call-done, bf16[4096,2048]{1,0:T(8,128)(2,1)} %all-gather.9.cloned.1.call-done), kind=kOutput, calls=%fused_computation.5 | convolution fusion | flops 17188257792 | bytes 37752832 | tf_op jit(solution)/shard_map/dot_general | solution.py:39
  337.3 10.2 %all-reduce.1 = (f32[1024]{0:T(1024)S(1)}, f32[1024]{0:T(1024)S(1)}) all-reduce(f32[1024]{0:T(1024)S(1)} %get-tuple-element.6, f32[1024]{0:T(1024)S(1)} %get-tuple-element.8), channel_id=1, replica_groups=mesh['teacher'=4,'student'=8] {'teacher'}, use_global_device_ids=true, to_apply=%region_3.4 | all-reduce | flops 2048 | bytes 16384 | tf_op jit(solution)/shard_map/psum | solution.py:46
  347.5 115.9 %all-gather.11.cloned.1.call-done = bf16[2048,4096]{0,1:T(8,128)(2,1)} async-done(((bf16[2048,512]{0,1:T(8,128)(2,1)}), bf16[2048,4096]{0,1:T(8,128)(2,1)}) %all-gather.11.cloned.1.call-update) | async-done | bytes 16777232 | tf_op jit(solution)/shard_map/all_gather | solution.py:44
  463.4 25.5 %convert_bitcast_fusion = bf16[4,1024,1024]{2,1,0:T(8,128)(2,1)} fusion(bf16[2048,4,1024]{0,2,1:T(8,128)(2,1)} %bitcast.61, f32[1024,2048]{1,0:T(8,128)} %get-tuple-element.7, bf16[1024,2048]{1,0:T(8,128)(2,1)} %param.11, f32[2048]{0:T(1024)S(1)} %convert_element_type.55, f32[1024]{0:T(1024)S(1)} %add_rsqrt_fusion), kind=kOutput, calls=%fused_computation.3 | convolution fusion | flops 17194549248 | bytes 37761024 | tf_op jit(solution)/shard_map/tf,fko->kto/dot_general | solution.py:63
  489.7 6.8 gather_fusion.2
  496.5 1.4 and_select_fusion
  497.9 3.3 all-to-all-start.1
  501.2 72.3 %reduce-scatter.7.cloned.1.call-done = bf16[1,1024,1024]{2,1,0:T(8,128)(2,1)} async-done(((bf16[4,1024,1024]{2,1,0:T(8,128)(2,1)}), bf16[1,1024,1024]{2,1,0:T(8,128)(2,1)}) %reduce-scatter.7.cloned.1.call-update) | async-done | bytes 2097168
  573.5 6.8 gather_fusion.1
  580.4 2.4 copy.29
  582.8 3.2 broadcast_select_fusion
  585.9 4.6 all-to-all-start
  590.6 48.9 %all-to-all-done = bf16[8,128,1024]{1,2,0:T(8,128)(2,1)S(1)} async-done(((bf16[8,128,1024]{1,2,0:T(8,128)(2,1)}), bf16[8,128,1024]{1,2,0:T(8,128)(2,1)S(1)}, u32[]{:S(2)}, u32[]{:S(2)}) %all-to-all-start) | async-done | bytes 2097184 | tf_op jit(solution)/shard_map/all_to_all | solution.py:72
  639.6 3.5 multiply_reduce_fusion.1
  643.1 8.9 %psum.30 = f32[1024]{0:T(1024)S(1)} all-reduce(f32[1024]{0:T(1024)S(1)} %get-tuple-element.3), channel_id=1, replica_groups=mesh['teacher'=4,'student'=8] {'teacher'}, use_global_device_ids=true, to_apply=%region_6.7 | all-reduce | flops 1024 | bytes 8192 | tf_op jit(solution)/shard_map/psum | solution.py:124
  652.0 10.5 %convolution_convert_fusion = bf16[2048,1024]{1,0:T(8,128)(2,1)} fusion(bf16[1024,2048]{0,1:T(8,128)(2,1)} %bitcast.52, f32[1024,1024]{0,1:T(8,128)} %get-tuple-element.9, f32[1024]{0:T(1024)S(1)} %broadcast_multiply_fusion, f32[1024]{0:T(1024)S(1)} %bitcast.57, f32[1024]{0:T(1024)S(1)} %convert_element_type.53, f32[1024]{0:T(1024)S(1)} %add_rsqrt_fusion.1, ...), kind=kOutput, calls=%fused_computation.19 | convolution fusion | flops 4307550208 | bytes 14696448 | tf_op jit(solution)/shard_map/dot_general | solution.py:130
  662.5 14.7 %psum.31 = f32[1024]{0:T(1024)} all-reduce(f32[1024]{0:T(1024)S(1)} %get-tuple-element.2), channel_id=1, replica_groups=mesh['teacher'=4,'student'=8] {'student'}, use_global_device_ids=true, to_apply=%region_9.10 | all-reduce | flops 1024 | bytes 8192 | tf_op jit(solution)/shard_map/psum | solution.py:137
  677.2 33.4 %reduce-scatter.5.cloned.1.call-done = bf16[256,1024]{1,0:T(8,128)(2,1)} async-done(((bf16[2048,1024]{1,0:T(8,128)(2,1)}), bf16[256,1024]{1,0:T(8,128)(2,1)}) %reduce-scatter.5.cloned.1.call-update) | async-done | bytes 524304 | tf_op jit(solution)/shard_map/reduce_scatter | solution.py:129
  710.7 2.1 convert_element_type.66
  (37 shorter events, 4.2 us)
Async XLA Ops:
  7.2 2.3 copy-start
  7.2 104.2 %all-gather.5.cloned.1.call-start = ((), (), s32[]{:S(2)}) async-start(), calls=%async_computation.4 | async-start | bytes 4718592 | tf_op jit(solution)/shard_map/all_gather | solution.py:111
  7.9 152.0 %all-gather.7.cloned.1.call-start = ((), (), s32[]{:S(2)}) async-start(), calls=%async_computation.5 | async-start | bytes 10485760 | tf_op jit(solution)/shard_map/all_gather | solution.py:37
  8.7 3.3 copy-start.1
  8.7 304.0 %all-gather.9.cloned.1.call-start = ((), (), s32[]{:S(2)}) async-start(), calls=%async_computation.6 | async-start | bytes 18874368 | tf_op jit(solution)/shard_map/all_gather | solution.py:41
  9.4 454.0 %all-gather.11.cloned.1.call-start = ((), (), s32[]{:S(2)}) async-start(), calls=%async_computation.7 | async-start | bytes 18874368 | tf_op jit(solution)/shard_map/all_gather | solution.py:44
  11.9 32.1 %copy-start.2 = (bf16[2048]{0:T(1024)(128)(2,1)S(1)}, bf16[2048]{0:T(1024)(128)(2,1)}, u32[]{:S(2)}) copy-start(bf16[2048]{0:T(1024)(128)(2,1)} %param.14) | copy-start | bytes 12292
  11.9 561.6 %reduce-scatter.7.cloned.1.call-start = ((), (), s32[]{:S(2)}) async-start(), calls=%async_computation.9 | async-start | bytes 10485760
  12.0 28.1 %collective-permute-start = (bf16[1024,512]{1,0:T(8,128)(2,1)S(1)}, bf16[1024,512]{1,0:T(8,128)(2,1)}, u32[]{:S(2)}, u32[]{:S(2)}) collective-permute-start(bf16[1024,512]{1,0:T(8,128)(2,1)S(1)} %copy-done.1), channel_id=1, source_target_pairs={{0,8},{8,16},{16,24},{24,0},{1,9},{9,17},{17,25},{25,1},{2,10},{10... | collective-permute-start | bytes 3145736 | tf_op jit(solution)/shard_map/ppermute | solution.py:94
  15.0 48.1 %collective-permute-start.2 = (bf16[1024,512]{1,0:T(8,128)(2,1)S(1)}, bf16[1024,512]{1,0:T(8,128)(2,1)}, u32[]{:S(2)}, u32[]{:S(2)}) collective-permute-start(bf16[1024,512]{1,0:T(8,128)(2,1)S(1)} %copy-done.1), channel_id=1, source_target_pairs={{8,0},{16,8},{24,16},{0,24},{9,1},{17,9},{25,17},{1,25},{10,2},{18... | collective-permute-start | bytes 3145736 | tf_op jit(solution)/shard_map/ppermute | solution.py:100
  40.1 56.5 %collective-permute-start.1 = (bf16[1024,512]{1,0:T(8,128)(2,1)}, bf16[1024,512]{1,0:T(8,128)(2,1)}, u32[]{:S(2)}, u32[]{:S(2)}) collective-permute-start(bf16[1024,512]{1,0:T(8,128)(2,1)} %collective-permute-done), channel_id=1, source_target_pairs={{0,8},{8,16},{16,24},{24,0},{1,9},{9,17},{17,25},{25,1},{2,10},{10... | collective-permute-start | bytes 3145736 | tf_op jit(solution)/shard_map/ppermute | solution.py:94
  488.9 0.8 copy-start.3
  497.9 88.0 %all-to-all-start.1 = ((bf16[8,1,128]{2,1,0:T(2,128)(2,1)}), bf16[8,1,128]{2,1,0:T(2,128)(2,1)S(1)}, u32[]{:S(2)}, u32[]{:S(2)}) async-start(bf16[8,1,128]{2,1,0:T(2,128)(2,1)} %and_select_fusion), calls=%async_computation.1 | async-start | bytes 8192 | tf_op jit(solution)/shard_map/all_to_all | solution.py:79
  582.8 7.8 %copy-start.4 = (bf16[1024]{0:T(1024)(128)(2,1)S(1)}, bf16[1024]{0:T(1024)(128)(2,1)}, u32[]{:S(2)}) copy-start(bf16[1024]{0:T(1024)(128)(2,1)} %param.19) | copy-start | bytes 6148
  585.9 53.6 %all-to-all-start = ((bf16[8,128,1024]{1,2,0:T(8,128)(2,1)}), bf16[8,128,1024]{1,2,0:T(8,128)(2,1)S(1)}, u32[]{:S(2)}, u32[]{:S(2)}) async-start(bf16[8,128,1024]{1,2,0:T(8,128)(2,1)} %broadcast_select_fusion), calls=%async_computation | async-start | bytes 4194304 | tf_op jit(solution)/shard_map/all_to_all | solution.py:72
  590.5 120.1 %reduce-scatter.5.cloned.1.call-start = ((), (), s32[]{:S(2)}) async-start(), calls=%async_computation.8 | async-start | bytes 4718592 | tf_op jit(solution)/shard_map/reduce_scatter | solution.py:129
Sparse Core Ops, SparseCore 0:
  9.6 49.5 all-gather.4
  61.0 98.8 all-gather.6
  161.5 151.0 all-gather.8
  314.1 149.2 all-gather.10
  489.0 84.4 reduce-scatter.6
  662.6 47.9 reduce-scatter.4
